TPU v7x, 256 devices: a whole 4x4x8 slice. The times are simulated.
256 devices in a mesh: ka: 32 (over y_hi, z, core), band: 8 (over y_lo, x).
Axes of the slice: x: 4, y: 4 (y_hi: 2, y_lo: 2; y = y_hi * 2 + y_lo), z: 8, core: 2. Of those that a mesh axis runs over, the one named last changes fastest.
Arguments:
- coefficients: bfloat16 [32, 2, 160, 2400], P('ka'), may hold values from -6 to 6
- class_weight: float32 [32], replicated, may hold values from 0.5 to 5
- diff_class: int32 [32, 32], replicated, may hold values from 0 to 31
- frag_cells: int32 [2], replicated, may hold values from 0 to 31
- block_pattern: int32 [2, 30], replicated, may hold values 0 or 1
Outputs:
- cluster: float32 [2, 2, 160, 2400], P(None, None, 'band', 'ka')
All inputs are finite; a program needn't handle non-finite values.
Results may differ from a plain program's by a relative error of at most 0.0017.
Values may be sent and summed in bfloat16 or wider, within the bound.
No kernel may reach another device: no remote copies, remote signals or barrier semaphores. Data moves between devices by JAX's collectives and lax.ppermute only.
A program may use at most 64 MiB of HBM per device.

v0:
```python
import jax
import jax.numpy as jnp
from jax import lax
from jax.sharding import PartitionSpec as P


def shards(coefficients, class_weight, diff_class, frag_cells, block_pattern):
    own_block = coefficients[0]
    occupied = own_block.shape[1]
    functions = own_block.shape[2]
    band_count = lax.axis_size("band")
    group_width = occupied // band_count
    kpoint_count = lax.axis_size("ka")
    kpoint_index = lax.axis_index("ka")
    high = lax.Precision.HIGHEST
    own_flat = own_block.reshape(2 * occupied, functions)
    my_group = lax.dynamic_slice_in_dim(
        own_block, lax.axis_index("band") * group_width, group_width, 1
    )
    diff_row = lax.dynamic_index_in_dim(diff_class, kpoint_index, 0, keepdims=False)
    classes = jnp.arange(class_weight.shape[0], dtype=jnp.int32)
    onehot = (diff_row[:, None] == classes[None, :]).astype(jnp.float32)
    weights = jnp.dot(onehot, class_weight, precision=high) / functions
    piece = lax.all_gather(my_group[None], "ka", axis=0, tiled=True)
    pieces = piece.shape[0]
    blocks = piece.reshape(pieces, 2 * group_width, functions)
    intersection = jnp.einsum("qia,ja->qij", blocks, own_flat, preferred_element_type=jnp.float32)
    m_real = intersection[:, :group_width, :occupied] + intersection[:, group_width:, occupied:]
    m_imag = intersection[:, :group_width, occupied:] - intersection[:, group_width:, :occupied]
    scaling = weights[:, None, None]
    m_real = (scaling * m_real).astype(jnp.bfloat16)
    m_imag = (scaling * m_imag).astype(jnp.bfloat16)
    m_block = jnp.concatenate(
        [jnp.concatenate([m_real, m_imag], 2), jnp.concatenate([-m_imag, m_real], 2)], 1
    )
    exchange = jnp.einsum("qio,qia->oa", m_block, blocks, preferred_element_type=jnp.float32)
    exchange = exchange.reshape(2, occupied, functions)
    phase_index = kpoint_index * frag_cells % kpoint_count
    angles = 2.0 * jnp.pi * phase_index.astype(jnp.float32) / kpoint_count
    cosines = (jnp.cos(angles) / kpoint_count)[:, None, None]
    sines = (jnp.sin(angles) / kpoint_count)[:, None, None]
    w_real = exchange[0][None]
    w_imag = exchange[1][None]
    terms = jnp.stack([cosines * w_real - sines * w_imag, sines * w_real + cosines * w_imag], 1)
    partial_value = lax.psum_scatter(terms, "band", scatter_dimension=2, tiled=True)
    cluster = lax.psum_scatter(partial_value, "ka", scatter_dimension=3, tiled=True)
    columns = cluster.shape[3]
    block_size = functions // block_pattern.shape[1]
    local_ids = (kpoint_index * columns + jnp.arange(columns, dtype=jnp.int32)) // block_size
    block_ids = jnp.arange(block_pattern.shape[1], dtype=jnp.int32)
    block_onehot = (block_ids[:, None] == local_ids[None, :]).astype(jnp.float32)
    block_mask = jnp.dot(block_pattern.astype(jnp.float32), block_onehot, precision=high)
    return cluster * block_mask[:, None, None, :]


def solution(mesh):
    placed = (P("ka", None, None, None), P(), P(), P(), P())
    return jax.shard_map(
        shards, mesh=mesh, in_specs=placed, out_specs=P(None, None, "band", "ka"), check_vma=False
    )
```

profile of v0, /device:TPU:1, one launch (start us, length us, event | category | flops | bytes accessed | tf_op | source)
XLA Modules:
  0.0 558.0 jit_solution(7503871566022568461)
XLA Ops:
  6.5 0.0 copy-start
  6.5 0.0 all-gather.2.cloned.1.call-start
  6.5 1.4 copy-done
  7.9 0.1 constant_dynamic-slice_fusion.1
  8.0 0.8 copy.19
  8.8 0.0 all-gather.2.cloned.1.call-update
  8.8 0.0 all-reduce.5.cloned.1.call-start
  8.9 0.7 dynamic-slice_bitcast_fusion
  9.6 0.7 cosine_multiply_fusion
  10.4 0.8 fusion
  11.2 97.5 %all-gather.2.cloned.1.call-done = bf16[32,2,20,2400]{3,1,2,0:T(2,128)(2,1)} async-done(((bf16[1,2,20,2400]{3,1,2,0:T(2,128)(2,1)}), bf16[32,2,20,2400]{3,1,2,0:T(2,128)(2,1)}) %all-gather.2.cloned.1.call-update) | async-done | bytes 6144016 | tf_op jit(solution)/shard_map/all_gather | solution.py:24
  108.7 3.5 copy.10
  112.2 3.5 fusion.24
  115.7 0.3 fusion.11
  116.0 0.3 fusion.21
  116.2 2.5 convolution_bitcast_fusion
  118.7 0.2 fusion.23
  118.9 6.8 %multiply_subtract_fusion = (f32[2,1,160,2400]{3,1,2,0:T(1,128)S(1)}, f32[2,1,160,2400]{3,1,2,0:T(1,128)}) fusion(f32[160,2400]{1,0:T(8,128)S(1)} %get-tuple-element.12, f32[160,2400]{1,0:T(8,128)S(1)} %get-tuple-element.11, f32[2]{0:T(128)S(1)} %sine_multiply_fusion, f32[2]{0:T(128)S(1)} %get-tuple-element.5), kind=kLoop, calls=%fused_computation.3 | loop fusion | flops 4608000 | bytes 9216016 | tf_op jit(solution)/shard_map/sub | solution.py:44
  125.7 10.2 %pad_maximum_fusion = f32[2,2,160,2400]{3,1,2,0:T(2,128)} fusion(f32[2,1,160,2400]{3,1,2,0:T(1,128)} %get-tuple-element.10, f32[2,1,160,2400]{3,1,2,0:T(1,128)S(1)} %get-tuple-element.9), kind=kLoop, calls=%fused_computation | loop fusion | flops 1536000 | bytes 12288000 | tf_op jit(solution)/shard_map/stack | solution.py:44
  135.9 0.0 all-reduce.5.cloned.1.call-update
  135.9 0.0 all-reduce.7.cloned.1.call-start
  136.0 0.6 copy-done.3
  136.6 0.6 dynamic-slice.1
  137.8 143.1 %all-reduce.5.cloned.1.call-done = f32[2,2,160,2400]{3,1,2,0:T(2,128)} async-done(((f32[2,2,160,2400]{3,1,2,0:T(2,128)}), f32[2,2,160,2400]{3,1,2,0:T(2,128)}) %all-reduce.5.cloned.1.call-update) | async-done | bytes 6144016
  280.9 2.1 constant_dynamic-slice_fusion
  283.0 0.0 all-reduce.7.cloned.1.call-update
  283.0 0.0 copy-done.2
  283.0 0.6 dynamic-slice.3
  284.3 0.0 copy-done.1
  284.3 0.1 convolution_bitcast_fusion.1
  284.4 265.5 %all-reduce.7.cloned.1.call-done = f32[2,2,20,2400]{3,1,2,0:T(2,128)} async-done(((f32[2,2,20,2400]{3,1,2,0:T(2,128)}), f32[2,2,20,2400]{3,1,2,0:T(2,128)}) %all-reduce.7.cloned.1.call-update) | async-done | bytes 768016
  549.9 1.6 dynamic-slice_multiply_fusion
  (5 shorter events, 0.1 us)
Async XLA Ops:
  6.5 1.4 copy-start
  6.5 102.2 %all-gather.2.cloned.1.call-start = ((), (), s32[]{:S(2)}) async-start(), calls=%async_computation | async-start | bytes 6420480 | tf_op jit(solution)/shard_map/all_gather | solution.py:24
  8.8 272.0 %all-reduce.5.cloned.1.call-start = ((), (), s32[]{:S(2)}) async-start(), calls=%async_computation.1 | async-start | bytes 12451840
  135.9 0.7 copy-start.3
  135.9 147.1 %copy-start.2 = (u32[256]{0:T(256)S(1)}, u32[256]{0:T(256)}, u32[]{:S(2)}) copy-start(u32[256]{0:T(256)} %constant.64) | copy-start | bytes 3076
  135.9 148.4 %copy-start.1 = (s32[2,30]{1,0:T(2,128)S(1)}, s32[2,30]{1,0:T(2,128)}, u32[]{:S(2)}) copy-start(s32[2,30]{1,0:T(2,128)} %param.9) | copy-start | bytes 724
  135.9 414.0 %all-reduce.7.cloned.1.call-start = ((), (), s32[]{:S(2)}) async-start(), calls=%async_computation.2 | async-start | bytes 1556480
Sparse Core Ops, SparseCore 0:
  10.1 98.5 all-gather.1
  136.0 144.7 all-reduce.4
  283.7 266.1 all-reduce.6
where the time goes:
time: 558 us
  waiting for transfers between devices  506 us (91%)
  other arithmetic  19.9 us (4%)
  between operations  14.5 us (3%)
  local copies, waits for them, and re-layouts  10.5 us (2%)
  matrix products  6.93 us (1%)
    unnamed x5, waiting for transfers between devices  409 us
    all_gather x1, waiting for transfers between devices, shards(): piece = lax.all_gather(my_group[None], 'ka', axis=0, tiled=True)  97.5 us
  transfers between devices with their start and end apart: 3, of which 3 were waited for; matrix products, arithmetic and copies ran while one was open for 1% of the time, Pallas kernels for 0%

commit v1 on v0

--- a/solution.py
+++ b/solution.py
@@ -21,7 +21,9 @@
     classes = jnp.arange(class_weight.shape[0], dtype=jnp.int32)
     onehot = (diff_row[:, None] == classes[None, :]).astype(jnp.float32)
     weights = jnp.dot(onehot, class_weight, precision=high) / functions
-    piece = lax.all_gather(my_group[None], "ka", axis=0, tiled=True)
+    own = my_group[None]
+    outgoing = jnp.stack([own] * lax.axis_size("ka"))
+    piece = jnp.concatenate(lax.all_to_all(outgoing, "ka", 0, 0), axis=0)
     pieces = piece.shape[0]
     blocks = piece.reshape(pieces, 2 * group_width, functions)
     intersection = jnp.einsum("qia,ja->qij", blocks, own_flat, preferred_element_type=jnp.float32)

time: 558 us -> 619 us (1.11)
  waiting for transfers between devices: 506 us -> 551 us
  starting transfers between devices: 0.09 us -> 13 us
    all_to_all x0 -> x1, waiting for transfers between devices: none -> 138 us  [shards(): piece = jnp.concatenate(lax.all_to_all(outgoing, 'ka', 0, 0), axis=0)]
    all_gather x1 -> x0, waiting for transfers between devices: 97.5 us -> none  [shards(): piece = lax.all_gather(my_group[None], 'ka', axis=0, tiled=True)]
    all_to_all x0 -> x1, starting transfers between devices: none -> 12.9 us  [shards(): piece = jnp.concatenate(lax.all_to_all(outgoing, 'ka', 0, 0), axis=0)]
    unnamed x5 -> x4, waiting for transfers between devices: 409 us -> 412 us
  transfers between devices with their start and end apart: 3 -> 3, of which waited for: 3 -> 3; matrix products, arithmetic and copies ran while one was open for 1% -> 0% of each run, Pallas kernels for 0% -> 0%
where the time goes in v1:
time: 619 us; the launch traced here: 618 us
  waiting for transfers between devices  551 us (89%)
  other arithmetic  19.2 us (3%)
  between operations  14.8 us (2%)
  local copies, waits for them, and re-layouts  14.3 us (2%)
  starting transfers between devices  13 us (2%)
  matrix products  6.27 us (1%)
    unnamed x4, waiting for transfers between devices  412 us
    all_to_all x1, waiting for transfers between devices, shards(): piece = jnp.concatenate(lax.all_to_all(outgoing, 'ka', 0, 0), axis=0)  138 us
    all_to_all x1, starting transfers between devices, shards(): piece = jnp.concatenate(lax.all_to_all(outgoing, 'ka', 0, 0), axis=0)  12.9 us
  transfers between devices with their start and end apart: 3, of which 3 were waited for; matrix products, arithmetic and copies ran while one was open for 0% of the time, Pallas kernels for 0%

profile of v1, /device:TPU:1, one launch (start us, length us, event | category | flops | bytes accessed | tf_op | source)
XLA Modules:
  0.0 618.4 jit_solution(5561305024788096667)
XLA Ops:
  6.5 0.0 copy-start
  6.5 1.4 copy-done
  7.9 0.1 constant_dynamic-slice_fusion.1
  8.0 0.2 copy.19
  8.2 4.4 stack.8
  12.6 12.9 %all-to-all-start = ((bf16[32,1,2,20,2400]{4,2,3,1,0:T(2,128)(2,1)}), bf16[32,1,2,20,2400]{4,2,3,1,0:T(2,128)(2,1)}, u32[]{:S(2)}, u32[]{:S(2)}) async-start(bf16[32,1,2,20,2400]{4,2,3,1,0:T(2,128)(2,1)} %stack.8), calls=%async_computation | async-start | bytes 12451840 | tf_op jit(solution)/shard_map/all_to_all | solution.py:26
  25.5 0.0 all-reduce.5.cloned.1.call-start
  25.6 0.7 dynamic-slice_bitcast_fusion
  26.3 0.0 copy-done.1
  26.3 0.1 cosine_multiply_fusion
  26.4 0.2 fusion
  26.6 138.4 %all-to-all-done = bf16[32,1,2,20,2400]{4,2,3,1,0:T(2,128)(2,1)} async-done(((bf16[32,1,2,20,2400]{4,2,3,1,0:T(2,128)(2,1)}), bf16[32,1,2,20,2400]{4,2,3,1,0:T(2,128)(2,1)}, u32[]{:S(2)}, u32[]{:S(2)}) %all-to-all-start) | async-done | bytes 6144032 | tf_op jit(solution)/shard_map/all_to_all | solution.py:26
  165.0 3.5 copy.13
  168.5 3.5 fusion.24
  172.0 0.3 fusion.11
  172.3 0.3 fusion.21
  172.5 2.5 convolution_bitcast_fusion
  175.0 0.2 fusion.23
  175.2 6.8 %multiply_subtract_fusion = (f32[2,1,160,2400]{3,1,2,0:T(1,128)S(1)}, f32[2,1,160,2400]{3,1,2,0:T(1,128)}) fusion(f32[160,2400]{1,0:T(8,128)S(1)} %get-tuple-element.12, f32[160,2400]{1,0:T(8,128)S(1)} %get-tuple-element.11, f32[2]{0:T(128)S(1)} %sine_multiply_fusion, f32[2]{0:T(128)S(1)} %get-tuple-element.5), kind=kLoop, calls=%fused_computation.3 | loop fusion | flops 4608000 | bytes 9216016 | tf_op jit(solution)/shard_map/sub | solution.py:46
  182.0 10.2 %pad_maximum_fusion = f32[2,2,160,2400]{3,1,2,0:T(2,128)} fusion(f32[2,1,160,2400]{3,1,2,0:T(1,128)} %get-tuple-element.10, f32[2,1,160,2400]{3,1,2,0:T(1,128)S(1)} %get-tuple-element.9), kind=kLoop, calls=%fused_computation | loop fusion | flops 1536000 | bytes 12288000 | tf_op jit(solution)/shard_map/stack | solution.py:46
  192.2 0.0 all-reduce.5.cloned.1.call-update
  192.2 0.0 all-reduce.7.cloned.1.call-start
  192.3 0.6 copy-done.5
  192.9 0.6 dynamic-slice.1
  194.1 146.9 %all-reduce.5.cloned.1.call-done = f32[2,2,160,2400]{3,1,2,0:T(2,128)} async-done(((f32[2,2,160,2400]{3,1,2,0:T(2,128)}), f32[2,2,160,2400]{3,1,2,0:T(2,128)}) %all-reduce.5.cloned.1.call-update) | async-done | bytes 6144016
  341.0 2.1 constant_dynamic-slice_fusion
  343.1 0.0 all-reduce.7.cloned.1.call-update
  343.1 0.6 dynamic-slice.3
  344.4 0.0 copy-done.2
  344.4 0.1 convolution_bitcast_fusion.1
  344.5 265.5 %all-reduce.7.cloned.1.call-done = f32[2,2,20,2400]{3,1,2,0:T(2,128)} async-done(((f32[2,2,20,2400]{3,1,2,0:T(2,128)}), f32[2,2,20,2400]{3,1,2,0:T(2,128)}) %all-reduce.7.cloned.1.call-update) | async-done | bytes 768016
  610.0 1.6 dynamic-slice_multiply_fusion
  (9 shorter events, 0.1 us)
Async XLA Ops:
  6.5 1.4 copy-start
  12.6 13.7 %copy-start.1 = (s32[2]{0:T(128)S(1)}, s32[2]{0:T(128)}, u32[]{:S(2)}) copy-start(s32[2]{0:T(128)} %param.8) | copy-start | bytes 28
  12.6 13.8 %copy-start.3 = (f32[32]{0:T(128)S(1)}, f32[32]{0:T(128)}, u32[]{:S(2)}) copy-start(f32[32]{0:T(128)} %param.6) | copy-start | bytes 388
  12.6 152.4 %all-to-all-start = ((bf16[32,1,2,20,2400]{4,2,3,1,0:T(2,128)(2,1)}), bf16[32,1,2,20,2400]{4,2,3,1,0:T(2,128)(2,1)}, u32[]{:S(2)}, u32[]{:S(2)}) async-start(bf16[32,1,2,20,2400]{4,2,3,1,0:T(2,128)(2,1)} %stack.8), calls=%async_computation | async-start | bytes 12451840 | tf_op jit(solution)/shard_map/all_to_all | solution.py:26
  25.5 315.4 %all-reduce.5.cloned.1.call-start = ((), (), s32[]{:S(2)}) async-start(), calls=%async_computation.1 | async-start | bytes 12451840
  192.2 0.7 copy-start.5
  192.2 150.9 %copy-start.4 = (u32[256]{0:T(256)S(1)}, u32[256]{0:T(256)}, u32[]{:S(2)}) copy-start(u32[256]{0:T(256)} %constant.64) | copy-start | bytes 3076
  192.2 152.2 %copy-start.2 = (s32[2,30]{1,0:T(2,128)S(1)}, s32[2,30]{1,0:T(2,128)}, u32[]{:S(2)}) copy-start(s32[2,30]{1,0:T(2,128)} %param.9) | copy-start | bytes 724
  192.2 417.8 %all-reduce.7.cloned.1.call-start = ((), (), s32[]{:S(2)}) async-start(), calls=%async_computation.2 | async-start | bytes 1556480
Sparse Core Ops, SparseCore 0:
  192.3 148.5 all-reduce.4
  343.8 266.1 all-reduce.6
